TPU v7x, 128 devices: a whole 4x4x4 slice. The times are simulated.
128 devices in a mesh: rows: 32 (over x, y, core), grp: 4 (over z).
Axes of the slice: x: 4, y: 4, z: 4, core: 2. Of those that a mesh axis runs over, the one named last changes fastest.
Arguments:
- embeddings: bfloat16 [262144, 1024], P('rows', 'grp'), may hold values from -6 to 6
- fine_local: int32 [262144], P('rows'), may hold values from 0 to 2047
- send_counts: int32 [32, 32], P('rows'), may hold values from 0 to 512, as said below
- old_fine: bfloat16 [65536, 1024], P('rows', 'grp'), may hold values from -6 to 6
- coarse_ids: int32 [65536], P('rows'), may hold values from 0 to 8191, as said below
- old_coarse: bfloat16 [8192, 1024], P('rows', 'grp'), may hold values from -6 to 6
Outputs:
- new_fine: bfloat16 [65536, 1024], P('rows', 'grp')
- coarse_dirs: bfloat16 [8192, 1024], P('rows')
Inputs may be any that keep to these rules, and one draw needn't show every extreme that they name: Row d of send_counts splits the 8192 rows of block d, in order, into segments for owners 0, 1, ...; each row of send_counts sums to 8192; one owner receives exactly 512 rows from every block. `coarse_ids`: within each block of 2048 consecutive level-1 clusters, at most 128 have a level-2 cluster in any one block of 256 consecutive level-2 clusters; one such block reaches that from every block.
All inputs are finite; a program needn't handle non-finite values.
Results may differ from a plain program's by a relative error of at most 0.006.
Values may be sent and summed in bfloat16 or wider, within the bound.
No kernel may reach another device: no remote copies, remote signals or barrier semaphores. Data moves between devices by JAX's collectives and lax.ppermute only.
A program may use at most 64 MiB of HBM per device.

v0:
```python
import math
import jax
import jax.numpy as jnp
from jax import lax
from jax.sharding import PartitionSpec as P


def onehot_sums(arrived, arrived_labels, fine_dev):
    slot_total = arrived.shape[0]
    width = arrived.shape[1]
    block_rows = math.gcd(slot_total, 2048)
    block_count = slot_total // block_rows
    cluster_index = jnp.arange(fine_dev, dtype=jnp.int32)

    def accumulate(state_pair, pieces):
        fine_sums, totals = state_pair
        row_block, label_block = pieces
        onehot = cluster_index[:, None] == label_block[None, :]
        fine_sums = fine_sums + jnp.dot(
            onehot.astype(jnp.bfloat16), row_block, preferred_element_type=jnp.float32
        )
        totals = totals + jnp.sum(onehot.astype(jnp.int32), axis=1)
        return ((fine_sums, totals), None)

    start_state = (jnp.zeros((fine_dev, width), jnp.float32), jnp.zeros((fine_dev,), jnp.int32))
    (fine_sums, totals), _ = lax.scan(
        accumulate,
        start_state,
        (
            arrived.reshape(block_count, block_rows, width),
            arrived_labels.reshape(block_count, block_rows),
        ),
    )
    return (fine_sums, totals.astype(jnp.float32))


def on_device(embeddings, fine_local, send_counts, old_fine, coarse_ids, old_coarse):
    peer_count = lax.axis_size("rows")
    per_dev = embeddings.shape[0]
    quarter = embeddings.shape[1]
    fine_dev = old_fine.shape[0]
    coarse_dev = old_coarse.shape[0]
    capacity = 2 * per_dev // peer_count
    counts = send_counts[0]
    starts = jnp.cumsum(counts) - counts
    offset = jnp.arange(capacity, dtype=jnp.int32)
    is_live = offset[None, :] < counts[:, None]
    padded_rows = jnp.concatenate(
        [embeddings, jnp.zeros((capacity, quarter), jnp.bfloat16)], axis=0
    )
    padded_local = jnp.concatenate([fine_local, jnp.zeros((capacity,), jnp.int32)], axis=0)

    def take_segment(first_row):
        segment_rows = lax.dynamic_slice_in_dim(padded_rows, first_row, capacity, 0)
        segment_labels = lax.dynamic_slice_in_dim(padded_local, first_row, capacity, 0)
        return (segment_rows, segment_labels)

    outgoing, raw_labels = lax.map(take_segment, starts)
    outgoing = jnp.where(is_live[:, :, None], outgoing, jnp.zeros((), jnp.bfloat16))
    labels = jnp.where(is_live, raw_labels, -1)
    arrived, arrived_labels = (
        lax.all_to_all(outgoing, "rows", split_axis=0, concat_axis=0, tiled=True),
        lax.all_to_all(labels, "rows", split_axis=0, concat_axis=0, tiled=True),
    )
    fine_sums, totals = onehot_sums(
        arrived.reshape(-1, quarter), arrived_labels.reshape(-1), fine_dev
    )
    new_fine = ((fine_sums + old_fine.astype(jnp.float32)) / (totals + 1.0)[:, None]).astype(
        jnp.bfloat16
    )
    owners = coarse_ids // coarse_dev
    local_id = coarse_ids - owners * coarse_dev
    capacity_two = 2 * fine_dev // peer_count
    member = (owners[:, None] == jnp.arange(peer_count, dtype=jnp.int32)[None, :]).astype(jnp.int32)
    slot_rank = jnp.sum(jnp.cumsum(member, axis=0) * member, axis=1) - 1
    slot_pos = owners * capacity_two + slot_rank
    placement = (
        jnp.arange(peer_count * capacity_two, dtype=jnp.int32)[:, None] == slot_pos[None, :]
    ).astype(jnp.bfloat16)
    outgoing_two = jnp.dot(placement, new_fine, preferred_element_type=jnp.float32).astype(
        jnp.bfloat16
    )
    label_plus = jnp.dot(
        placement, (local_id + 1).astype(jnp.bfloat16), preferred_element_type=jnp.float32
    )
    labels_two = label_plus.astype(jnp.int32) - 1
    received, received_labels = (
        lax.all_to_all(
            outgoing_two.reshape(peer_count, capacity_two, quarter),
            "rows",
            split_axis=0,
            concat_axis=0,
            tiled=True,
        ),
        lax.all_to_all(
            labels_two.reshape(peer_count, capacity_two),
            "rows",
            split_axis=0,
            concat_axis=0,
            tiled=True,
        ),
    )
    onehot_two = (
        jnp.arange(coarse_dev, dtype=jnp.int32)[:, None] == received_labels.reshape(-1)[None, :]
    )
    coarse_sums = jnp.dot(
        onehot_two.astype(jnp.bfloat16),
        received.reshape(-1, quarter),
        preferred_element_type=jnp.float32,
    )
    coarse_totals = jnp.sum(onehot_two.astype(jnp.int32), axis=1).astype(jnp.float32)
    coarse_means = (coarse_sums + old_coarse.astype(jnp.float32)) / (coarse_totals + 1.0)[:, None]
    full_means = lax.all_gather(coarse_means, "grp", axis=1, tiled=True)
    scale = lax.rsqrt(jnp.mean(full_means * full_means, axis=1, keepdims=True) + 1e-06)
    coarse_dirs = (full_means * scale).astype(jnp.bfloat16)
    return (new_fine, coarse_dirs)


def solution(mesh):
    in_specs = (
        P("rows", "grp"),
        P("rows"),
        P("rows", None),
        P("rows", "grp"),
        P("rows"),
        P("rows", "grp"),
    )
    out_specs = (P("rows", "grp"), P("rows", None))
    return jax.shard_map(
        on_device, mesh=mesh, in_specs=in_specs, out_specs=out_specs, check_vma=False
    )
```

profile of v0, /device:TPU:0, one launch (start us, length us, event | category | flops | bytes accessed | tf_op | source)
XLA Modules:
  0.0 446.7 jit_solution(14028012184819032292)
XLA Ops:
  9.5 3.9 concatenate.6
  13.4 147.6 %while.27 = (s32[]{:T(128)}, bf16[32,512,256]{2,1,0:T(8,128)(2,1)}, s32[32,512]{1,0:T(8,128)S(1)}, s32[32]{0:T(128)S(1)}, bf16[8704,256]{1,0:T(8,128)(2,1)}, /*index=5*/s32[8704]{0:T(1024)S(1)}) while((s32[]{:T(128)}, bf16[32,512,256]{2,1,0:T(8,128)(2,1)}, s32[32,512]{1,0:T(8,128)S(1)}, s32[32]{0:T(128)S(1)}, ...), condition=%wide.region_2.3_spmd.clone, body=%wide.region_1.2_spmd.sunk.clone | while | flops 5 | bytes 533119 | solution.py:58
  29.9 1.7 bitcast_dynamic-update-slice_fusion.3
  34.6 1.7 bitcast_dynamic-update-slice_fusion.3
  39.2 1.7 bitcast_dynamic-update-slice_fusion.3
  48.4 1.7 bitcast_dynamic-update-slice_fusion.3
  53.0 1.7 bitcast_dynamic-update-slice_fusion.3
  66.9 1.7 bitcast_dynamic-update-slice_fusion.3
  71.5 1.7 bitcast_dynamic-update-slice_fusion.3
  76.1 1.7 bitcast_dynamic-update-slice_fusion.3
  85.4 1.7 bitcast_dynamic-update-slice_fusion.3
  99.2 1.7 bitcast_dynamic-update-slice_fusion.3
  103.8 1.7 bitcast_dynamic-update-slice_fusion.3
  113.0 1.7 bitcast_dynamic-update-slice_fusion.3
  117.7 1.7 bitcast_dynamic-update-slice_fusion.3
  122.3 1.7 bitcast_dynamic-update-slice_fusion.3
  136.1 1.7 bitcast_dynamic-update-slice_fusion.3
  140.7 1.7 bitcast_dynamic-update-slice_fusion.3
  159.2 1.7 bitcast_dynamic-update-slice_fusion.3
  161.8 7.4 %all-to-all-start = ((s32[32,1,512]{2,1,0:T(1,128)}), s32[32,1,512]{2,1,0:T(1,128)S(1)}, u32[]{:S(2)}, u32[]{:S(2)}) async-start(s32[32,1,512]{2,1,0:T(1,128)} %all_to_all.18), calls=%async_computation | async-start | bytes 131072 | tf_op jit(solution)/shard_map/all_to_all | solution.py:63
  169.3 8.1 %broadcast_select_fusion = bf16[32,512,256]{2,1,0:T(8,128)(2,1)} fusion(bf16[32,512,256]{2,1,0:T(8,128)(2,1)} %get-tuple-element.69, pred[32,512]{1,0:T(8,128)(4,1)S(1)} %iota_compare_fusion.17), kind=kLoop, calls=%fused_computation.18 | loop fusion | flops 4194304 | bytes 16793600 | tf_op jit(solution)/shard_map/jit(_where)/select_n | solution.py:59
  177.4 7.6 %all-to-all-start.1 = ((bf16[32,512,256]{2,1,0:T(8,128)(2,1)}), bf16[32,512,256]{2,1,0:T(8,128)(2,1)}, u32[]{:S(2)}, u32[]{:S(2)}) async-start(bf16[32,512,256]{2,1,0:T(8,128)(2,1)} %broadcast_select_fusion), calls=%async_computation.1 | async-start | bytes 16777216 | tf_op jit(solution)/shard_map/all_to_all | solution.py:62
  185.1 9.1 %reduce-window.20 = s32[32,16,128]{2,1,0:T(8,128)S(1)} reduce-window(s32[32,16,128]{2,1,0:T(8,128)S(1)} %fusion.21, s32[]{:T(128)} %copy.41), window={size=1x1x128 pad=0_0x0_0x127_0}, to_apply=%region_6.7 | reduce-window | flops 8323072 | bytes 524292 | tf_op jit(solution)/shard_map/reduce-window.1
  195.1 5.6 %fusion.11 = f32[1,4096]{1,0:T(1,128)S(1)} fusion(bf16[2048,1]{0,1:T(2,128)(2,1)S(1)} %reshape.106, s32[2048]{0:T(1024)S(1)} %get-tuple-element.115), kind=kOutput, calls=%fused_computation.15 | convolution fusion | flops 25165824 | bytes 28672 | tf_op jit(solution)/shard_map/dot_general | solution.py:83
  201.5 97.1 %all-to-all-done.1 = bf16[32,512,256]{2,1,0:T(8,128)(2,1)} async-done(((bf16[32,512,256]{2,1,0:T(8,128)(2,1)}), bf16[32,512,256]{2,1,0:T(8,128)(2,1)}, u32[]{:S(2)}, u32[]{:S(2)}) %all-to-all-start.1) | async-done | bytes 8388640 | tf_op jit(solution)/shard_map/all_to_all | solution.py:62
  298.6 14.2 %all-to-all-start.2 = ((s32[32,1,128]{2,1,0:T(1,128)}), s32[32,1,128]{2,1,0:T(1,128)S(1)}, u32[]{:S(2)}, u32[]{:S(2)}) async-start(s32[32,1,128]{2,1,0:T(1,128)} %bitcast.11), calls=%async_computation.2 | async-start | bytes 32768 | tf_op jit(solution)/shard_map/all_to_all | solution.py:95
  312.8 54.2 %while.28 = (s32[]{:T(128)}, f32[2048,256]{1,0:T(8,128)S(1)}, s32[2048]{0:T(1024)S(1)}, s32[8,2048]{1,0:T(8,128)S(1)}, bf16[8,2048,256]{2,1,0:T(8,128)(2,1)}) while((s32[]{:T(128)}, f32[2048,256]{1,0:T(8,128)S(1)}, s32[2048]{0:T(1024)S(1)}, s32[8,2048]{1,0:T(8,128)S(1)}, bf16[8,2048,256]{2,1,0:T(8,128)(2,1)}) %tuple.50), condition=%wide.region_5.6_spmd.clone.clone, body=%wide.region_3.5_spmd.clone.sunk.clone | while | flops 2165311488 | bytes 5309004 | solution.py:26
  312.8 5.1 %fusion.35 = f32[2048,256]{1,0:T(8,128)S(1)} fusion(s32[2048]{0:T(1024)S(1)} %bitcast.55, f32[2048,256]{1,0:T(8,128)S(1)} %get-tuple-element.239, bf16[8,2048,256]{2,1,0:T(8,128)(2,1)} %get-tuple-element.247, s32[]{:T(128)} %get-tuple-element.238, pred[]{:T(512)S(6)} %compare.8), kind=kOutput, calls=%fused_computation.7.clone.1.clone | convolution fusion | flops 2152726528 | bytes 5251585 | tf_op jit(solution)/shard_map/while/body/eval_jaxpr/dot_general | solution.py:19
  317.9 1.7 fusion.36
  319.7 5.0 %fusion.35 = f32[2048,256]{1,0:T(8,128)S(1)} fusion(s32[2048]{0:T(1024)S(1)} %bitcast.55, f32[2048,256]{1,0:T(8,128)S(1)} %get-tuple-element.239, bf16[8,2048,256]{2,1,0:T(8,128)(2,1)} %get-tuple-element.247, s32[]{:T(128)} %get-tuple-element.238, pred[]{:T(512)S(6)} %compare.8), kind=kOutput, calls=%fused_computation.7.clone.1.clone | convolution fusion | flops 2152726528 | bytes 5251585 | tf_op jit(solution)/shard_map/while/body/eval_jaxpr/dot_general | solution.py:19
  324.7 1.7 fusion.36
  326.4 5.0 %fusion.35 = f32[2048,256]{1,0:T(8,128)S(1)} fusion(s32[2048]{0:T(1024)S(1)} %bitcast.55, f32[2048,256]{1,0:T(8,128)S(1)} %get-tuple-element.239, bf16[8,2048,256]{2,1,0:T(8,128)(2,1)} %get-tuple-element.247, s32[]{:T(128)} %get-tuple-element.238, pred[]{:T(512)S(6)} %compare.8), kind=kOutput, calls=%fused_computation.7.clone.1.clone | convolution fusion | flops 2152726528 | bytes 5251585 | tf_op jit(solution)/shard_map/while/body/eval_jaxpr/dot_general | solution.py:19
  331.4 1.7 fusion.36
  333.2 5.0 %fusion.35 = f32[2048,256]{1,0:T(8,128)S(1)} fusion(s32[2048]{0:T(1024)S(1)} %bitcast.55, f32[2048,256]{1,0:T(8,128)S(1)} %get-tuple-element.239, bf16[8,2048,256]{2,1,0:T(8,128)(2,1)} %get-tuple-element.247, s32[]{:T(128)} %get-tuple-element.238, pred[]{:T(512)S(6)} %compare.8), kind=kOutput, calls=%fused_computation.7.clone.1.clone | convolution fusion | flops 2152726528 | bytes 5251585 | tf_op jit(solution)/shard_map/while/body/eval_jaxpr/dot_general | solution.py:19
  338.2 1.7 fusion.36
  340.0 5.0 %fusion.35 = f32[2048,256]{1,0:T(8,128)S(1)} fusion(s32[2048]{0:T(1024)S(1)} %bitcast.55, f32[2048,256]{1,0:T(8,128)S(1)} %get-tuple-element.239, bf16[8,2048,256]{2,1,0:T(8,128)(2,1)} %get-tuple-element.247, s32[]{:T(128)} %get-tuple-element.238, pred[]{:T(512)S(6)} %compare.8), kind=kOutput, calls=%fused_computation.7.clone.1.clone | convolution fusion | flops 2152726528 | bytes 5251585 | tf_op jit(solution)/shard_map/while/body/eval_jaxpr/dot_general | solution.py:19
  345.0 1.7 fusion.36
  346.7 5.0 %fusion.35 = f32[2048,256]{1,0:T(8,128)S(1)} fusion(s32[2048]{0:T(1024)S(1)} %bitcast.55, f32[2048,256]{1,0:T(8,128)S(1)} %get-tuple-element.239, bf16[8,2048,256]{2,1,0:T(8,128)(2,1)} %get-tuple-element.247, s32[]{:T(128)} %get-tuple-element.238, pred[]{:T(512)S(6)} %compare.8), kind=kOutput, calls=%fused_computation.7.clone.1.clone | convolution fusion | flops 2152726528 | bytes 5251585 | tf_op jit(solution)/shard_map/while/body/eval_jaxpr/dot_general | solution.py:19
  351.7 1.7 fusion.36
  353.5 5.0 %fusion.35 = f32[2048,256]{1,0:T(8,128)S(1)} fusion(s32[2048]{0:T(1024)S(1)} %bitcast.55, f32[2048,256]{1,0:T(8,128)S(1)} %get-tuple-element.239, bf16[8,2048,256]{2,1,0:T(8,128)(2,1)} %get-tuple-element.247, s32[]{:T(128)} %get-tuple-element.238, pred[]{:T(512)S(6)} %compare.8), kind=kOutput, calls=%fused_computation.7.clone.1.clone | convolution fusion | flops 2152726528 | bytes 5251585 | tf_op jit(solution)/shard_map/while/body/eval_jaxpr/dot_general | solution.py:19
  358.5 1.7 fusion.36
  360.3 5.0 %fusion.35 = f32[2048,256]{1,0:T(8,128)S(1)} fusion(s32[2048]{0:T(1024)S(1)} %bitcast.55, f32[2048,256]{1,0:T(8,128)S(1)} %get-tuple-element.239, bf16[8,2048,256]{2,1,0:T(8,128)(2,1)} %get-tuple-element.247, s32[]{:T(128)} %get-tuple-element.238, pred[]{:T(512)S(6)} %compare.8), kind=kOutput, calls=%fused_computation.7.clone.1.clone | convolution fusion | flops 2152726528 | bytes 5251585 | tf_op jit(solution)/shard_map/while/body/eval_jaxpr/dot_general | solution.py:19
  365.2 1.7 fusion.36
  368.4 7.4 %fusion.14 = bf16[4096,256]{1,0:T(8,128)(2,1)} fusion(bf16[2048,256]{1,0:T(8,128)(2,1)S(1)} %divide_convert_fusion, s32[2048]{0:T(1024)S(1)} %get-tuple-element.115), kind=kOutput, calls=%fused_computation.19 | convolution fusion | flops 4304404480 | bytes 3153920 | tf_op jit(solution)/shard_map/dot_general | solution.py:80
  375.8 7.3 %all-to-all-start.3 = ((bf16[32,128,256]{2,1,0:T(8,128)(2,1)}), bf16[32,128,256]{2,1,0:T(8,128)(2,1)S(1)}, u32[]{:S(2)}, u32[]{:S(2)}) async-start(bf16[32,128,256]{2,1,0:T(8,128)(2,1)} %bitcast.13), calls=%async_computation.3 | async-start | bytes 4194304 | tf_op jit(solution)/shard_map/all_to_all | solution.py:88
  383.7 28.4 %all-to-all-done.3 = bf16[32,128,256]{2,1,0:T(8,128)(2,1)S(1)} async-done(((bf16[32,128,256]{2,1,0:T(8,128)(2,1)}), bf16[32,128,256]{2,1,0:T(8,128)(2,1)S(1)}, u32[]{:S(2)}, u32[]{:S(2)}) %all-to-all-start.3) | async-done | bytes 2097184 | tf_op jit(solution)/shard_map/all_to_all | solution.py:88
  413.6 22.8 %all-gather.2.cloned.1.call-done = f32[256,1024]{1,0:T(8,128)} async-done(((f32[256,256]{1,0:T(8,128)}), f32[256,1024]{1,0:T(8,128)}) %all-gather.2.cloned.1.call-update) | async-done | bytes 1048592 | tf_op jit(solution)/shard_map/all_gather | solution.py:113
  437.7 2.1 multiply_convert_fusion
  (172 shorter events, 60.5 us)
Async XLA Ops:
  9.5 151.5 %copy-start.3 = (s32[1,32]{1,0:T(1,128)S(1)}, s32[1,32]{1,0:T(1,128)}, u32[]{:S(2)}) copy-start(s32[1,32]{1,0:T(1,128)} %param.12) | copy-start | bytes 388
  161.8 15.6 %all-to-all-start = ((s32[32,1,512]{2,1,0:T(1,128)}), s32[32,1,512]{2,1,0:T(1,128)S(1)}, u32[]{:S(2)}, u32[]{:S(2)}) async-start(s32[32,1,512]{2,1,0:T(1,128)} %all_to_all.18), calls=%async_computation | async-start | bytes 131072 | tf_op jit(solution)/shard_map/all_to_all | solution.py:63
  177.4 7.7 %copy-start.2 = (s32[2048]{0:T(1024)S(1)}, s32[2048]{0:T(1024)}, u32[]{:S(2)}) copy-start(s32[2048]{0:T(1024)} %param.14) | copy-start | bytes 24580
  177.4 121.2 %all-to-all-start.1 = ((bf16[32,512,256]{2,1,0:T(8,128)(2,1)}), bf16[32,512,256]{2,1,0:T(8,128)(2,1)}, u32[]{:S(2)}, u32[]{:S(2)}) async-start(bf16[32,512,256]{2,1,0:T(8,128)(2,1)} %broadcast_select_fusion), calls=%async_computation.1 | async-start | bytes 16777216 | tf_op jit(solution)/shard_map/all_to_all | solution.py:62
  298.6 77.3 %all-to-all-start.2 = ((s32[32,1,128]{2,1,0:T(1,128)}), s32[32,1,128]{2,1,0:T(1,128)S(1)}, u32[]{:S(2)}, u32[]{:S(2)}) async-start(s32[32,1,128]{2,1,0:T(1,128)} %bitcast.11), calls=%async_computation.2 | async-start | bytes 32768 | tf_op jit(solution)/shard_map/all_to_all | solution.py:95
  312.8 54.2 %copy-start = (bf16[2048,256]{1,0:T(8,128)(2,1)S(1)}, bf16[2048,256]{1,0:T(8,128)(2,1)}, u32[]{:S(2)}) copy-start(bf16[2048,256]{1,0:T(8,128)(2,1)} %param.13) | copy-start | bytes 3145732
  367.4 1.0 copy-start.1
  375.8 36.3 %copy-start.4 = (bf16[256,256]{1,0:T(8,128)(2,1)S(1)}, bf16[256,256]{1,0:T(8,128)(2,1)}, u32[]{:S(2)}) copy-start(bf16[256,256]{1,0:T(8,128)(2,1)} %param.15) | copy-start | bytes 393220
  375.8 36.3 %all-to-all-start.3 = ((bf16[32,128,256]{2,1,0:T(8,128)(2,1)}), bf16[32,128,256]{2,1,0:T(8,128)(2,1)S(1)}, u32[]{:S(2)}, u32[]{:S(2)}) async-start(bf16[32,128,256]{2,1,0:T(8,128)(2,1)} %bitcast.13), calls=%async_computation.3 | async-start | bytes 4194304 | tf_op jit(solution)/shard_map/all_to_all | solution.py:88
  383.2 53.1 %all-gather.2.cloned.1.call-start = ((), (), s32[]{:S(2)}) async-start(), calls=%async_computation.4 | async-start | bytes 1310720 | tf_op jit(solution)/shard_map/all_gather | solution.py:113
Sparse Core Ops, SparseCore 0:
  413.7 22.5 all-gather.1
where the time goes:
time: 450 us; the launch traced here: 447 us
  waiting for transfers between devices  148 us (33%)
  local copies, waits for them, and re-layouts  87.8 us (20%)
  loops' own time  67.7 us (15%)
  matrix products  54.3 us (12%)
  other arithmetic  37.7 us (8%)
  starting transfers between devices  36.7 us (8%)
  between operations  14.2 us (3%)
    all_to_all x1, waiting for transfers between devices, on_device(): lax.all_to_all(outgoing, 'rows', split_axis=0, concat_axis=0, tiled=True)  97.1 us
    another operation x1, loops' own time, on_device(): outgoing, raw_labels = lax.map(take_segment, starts)  67.3 us
    dynamic_update_slice x64, local copies, waits for them, and re-layouts, on_device(): outgoing, raw_labels = lax.map(take_segment, starts)  56.5 us
    dot_general x8, matrix products, accumulate(): jnp.dot(onehot.astype(jnp.bfloat16), row_block, preferred_element_type=jn...  39.8 us
    all_to_all x1, waiting for transfers between devices, on_device(): lax.all_to_all(outgoing_two.reshape(peer_count, capacity_two, quarter), '...  28.4 us
    all_gather x1, waiting for transfers between devices, on_device(): full_means = lax.all_gather(coarse_means, 'grp', axis=1, tiled=True)  22.8 us
    dynamic_slice x32, local copies, waits for them, and re-layouts, on_device(): outgoing, raw_labels = lax.map(take_segment, starts)  21.4 us
    all_to_all x1, starting transfers between devices, on_device(): lax.all_to_all(labels_two.reshape(peer_count, capacity_two), 'rows', spli...  14.2 us
  transfers between devices with their start and end apart: 5, of which 3 were waited for; matrix products, arithmetic and copies ran while one was open for 19% of the time, Pallas kernels for 0%

commit v1 on v0

--- a/solution.py
+++ b/solution.py
@@ -110,7 +110,9 @@
     )
     coarse_totals = jnp.sum(onehot_two.astype(jnp.int32), axis=1).astype(jnp.float32)
     coarse_means = (coarse_sums + old_coarse.astype(jnp.float32)) / (coarse_totals + 1.0)[:, None]
-    full_means = lax.all_gather(coarse_means, "grp", axis=1, tiled=True)
+    full_means = jnp.concatenate(
+        lax.all_to_all(jnp.stack([coarse_means] * lax.axis_size("grp")), "grp", 0, 0), axis=1
+    )
     scale = lax.rsqrt(jnp.mean(full_means * full_means, axis=1, keepdims=True) + 1e-06)
     coarse_dirs = (full_means * scale).astype(jnp.bfloat16)
     return (new_fine, coarse_dirs)

time: 450 us -> 431 us (0.958)
  waiting for transfers between devices: 148 us -> 126 us
  blocking collectives: 0 us -> 20.1 us
  between operations: 14.2 us -> 0.87 us
    all_gather x1 -> x0, waiting for transfers between devices: 22.8 us -> none  [on_device(): full_means = lax.all_gather(coarse_means, 'grp', axis=1, tiled=True)]
    all_to_all x0 -> x1, blocking collectives: none -> 20.1 us  [on_device(): lax.all_to_all(jnp.stack([coarse_means] * lax.axis_size('grp')), 'grp', 0...]
  transfers between devices with their start and end apart: 5 -> 4, of which waited for: 3 -> 2; matrix products, arithmetic and copies ran while one was open for 19% -> 20% of each run, Pallas kernels for 0% -> 0%
where the time goes in v1:
time: 431 us; the launch traced here: 428 us
  waiting for transfers between devices  126 us (29%)
  local copies, waits for them, and re-layouts  89.2 us (21%)
  loops' own time  67.7 us (16%)
  matrix products  53.6 us (12%)
  starting transfers between devices  36.7 us (9%)
  other arithmetic  34.5 us (8%)
  blocking collectives  20.1 us (5%)
    all_to_all x1, waiting for transfers between devices, on_device(): lax.all_to_all(outgoing, 'rows', split_axis=0, concat_axis=0, tiled=True)  97.1 us
    another operation x1, loops' own time, on_device(): outgoing, raw_labels = lax.map(take_segment, starts)  67.3 us
    dynamic_update_slice x64, local copies, waits for them, and re-layouts, on_device(): outgoing, raw_labels = lax.map(take_segment, starts)  56.5 us
    dot_general x8, matrix products, accumulate(): jnp.dot(onehot.astype(jnp.bfloat16), row_block, preferred_element_type=jn...  39.8 us
    all_to_all x1, waiting for transfers between devices, on_device(): lax.all_to_all(outgoing_two.reshape(peer_count, capacity_two, quarter), '...  28.4 us
    dynamic_slice x32, local copies, waits for them, and re-layouts, on_device(): outgoing, raw_labels = lax.map(take_segment, starts)  21.4 us
    all_to_all x1, blocking collectives, on_device(): lax.all_to_all(jnp.stack([coarse_means] * lax.axis_size('grp')), 'grp', 0...  20.1 us
    all_to_all x1, starting transfers between devices, on_device(): lax.all_to_all(labels_two.reshape(peer_count, capacity_two), 'rows', spli...  14.2 us
  transfers between devices with their start and end apart: 4, of which 2 were waited for; matrix products, arithmetic and copies ran while one was open for 20% of the time, Pallas kernels for 0%

profile of v1, /device:TPU:0, one launch (start us, length us, event | category | flops | bytes accessed | tf_op | source)
XLA Modules:
  0.0 428.1 jit_solution(3371059451216407386)
XLA Ops:
  3.0 3.9 concatenate.6
  6.9 147.6 %while.27 = (s32[]{:T(128)}, bf16[32,512,256]{2,1,0:T(8,128)(2,1)}, s32[32,512]{1,0:T(8,128)S(1)}, s32[32]{0:T(128)S(1)}, bf16[8704,256]{1,0:T(8,128)(2,1)}, /*index=5*/s32[8704]{0:T(1024)S(1)}) while((s32[]{:T(128)}, bf16[32,512,256]{2,1,0:T(8,128)(2,1)}, s32[32,512]{1,0:T(8,128)S(1)}, s32[32]{0:T(128)S(1)}, ...), condition=%wide.region_2.3_spmd.clone, body=%wide.region_1.2_spmd.sunk.clone | while | flops 5 | bytes 533119 | solution.py:58
  23.4 1.7 bitcast_dynamic-update-slice_fusion.3
  28.0 1.7 bitcast_dynamic-update-slice_fusion.3
  32.7 1.7 bitcast_dynamic-update-slice_fusion.3
  41.9 1.7 bitcast_dynamic-update-slice_fusion.3
  46.5 1.7 bitcast_dynamic-update-slice_fusion.3
  60.4 1.7 bitcast_dynamic-update-slice_fusion.3
  65.0 1.7 bitcast_dynamic-update-slice_fusion.3
  69.6 1.7 bitcast_dynamic-update-slice_fusion.3
  78.8 1.7 bitcast_dynamic-update-slice_fusion.3
  92.6 1.7 bitcast_dynamic-update-slice_fusion.3
  97.3 1.7 bitcast_dynamic-update-slice_fusion.3
  101.9 1.7 bitcast_dynamic-update-slice_fusion.3
  106.5 1.7 bitcast_dynamic-update-slice_fusion.3
  111.1 1.7 bitcast_dynamic-update-slice_fusion.3
  115.7 1.7 bitcast_dynamic-update-slice_fusion.3
  129.6 1.7 bitcast_dynamic-update-slice_fusion.3
  134.2 1.7 bitcast_dynamic-update-slice_fusion.3
  152.6 1.7 bitcast_dynamic-update-slice_fusion.3
  155.3 7.4 %all-to-all-start = ((s32[32,1,512]{2,1,0:T(1,128)}), s32[32,1,512]{2,1,0:T(1,128)S(1)}, u32[]{:S(2)}, u32[]{:S(2)}) async-start(s32[32,1,512]{2,1,0:T(1,128)} %all_to_all.21), calls=%async_computation | async-start | bytes 131072 | tf_op jit(solution)/shard_map/all_to_all | solution.py:63
  162.8 8.1 %broadcast_select_fusion = bf16[32,512,256]{2,1,0:T(8,128)(2,1)} fusion(bf16[32,512,256]{2,1,0:T(8,128)(2,1)} %get-tuple-element.69, pred[32,512]{1,0:T(8,128)(4,1)S(1)} %iota_compare_fusion.17), kind=kLoop, calls=%fused_computation.18 | loop fusion | flops 4194304 | bytes 16793600 | tf_op jit(solution)/shard_map/jit(_where)/select_n | solution.py:59
  170.9 7.7 %all-to-all-start.1 = ((bf16[32,512,256]{2,1,0:T(8,128)(2,1)}), bf16[32,512,256]{2,1,0:T(8,128)(2,1)}, u32[]{:S(2)}, u32[]{:S(2)}) async-start(bf16[32,512,256]{2,1,0:T(8,128)(2,1)} %broadcast_select_fusion), calls=%async_computation.1 | async-start | bytes 16777216 | tf_op jit(solution)/shard_map/all_to_all | solution.py:62
  178.6 9.1 %reduce-window.20 = s32[32,16,128]{2,1,0:T(8,128)S(1)} reduce-window(s32[32,16,128]{2,1,0:T(8,128)S(1)} %fusion.23, s32[]{:T(128)} %copy.48), window={size=1x1x128 pad=0_0x0_0x127_0}, to_apply=%region_6.7 | reduce-window | flops 8323072 | bytes 524292 | tf_op jit(solution)/shard_map/reduce-window.1
  188.5 5.6 %fusion.11 = f32[1,4096]{1,0:T(1,128)S(1)} fusion(bf16[2048,1]{0,1:T(2,128)(2,1)S(1)} %reshape.116, s32[2048]{0:T(1024)S(1)} %get-tuple-element.119), kind=kOutput, calls=%fused_computation.15 | convolution fusion | flops 25165824 | bytes 28672 | tf_op jit(solution)/shard_map/dot_general | solution.py:83
  194.9 97.1 %all-to-all-done.1 = bf16[32,512,256]{2,1,0:T(8,128)(2,1)} async-done(((bf16[32,512,256]{2,1,0:T(8,128)(2,1)}), bf16[32,512,256]{2,1,0:T(8,128)(2,1)}, u32[]{:S(2)}, u32[]{:S(2)}) %all-to-all-start.1) | async-done | bytes 8388640 | tf_op jit(solution)/shard_map/all_to_all | solution.py:62
  292.0 14.2 %all-to-all-start.2 = ((s32[32,1,128]{2,1,0:T(1,128)}), s32[32,1,128]{2,1,0:T(1,128)S(1)}, u32[]{:S(2)}, u32[]{:S(2)}) async-start(s32[32,1,128]{2,1,0:T(1,128)} %bitcast.11), calls=%async_computation.2 | async-start | bytes 32768 | tf_op jit(solution)/shard_map/all_to_all | solution.py:95
  306.3 54.2 %while.28 = (s32[]{:T(128)}, f32[2048,256]{1,0:T(8,128)S(1)}, s32[2048]{0:T(1024)S(1)}, s32[8,2048]{1,0:T(8,128)S(1)}, bf16[8,2048,256]{2,1,0:T(8,128)(2,1)}) while((s32[]{:T(128)}, f32[2048,256]{1,0:T(8,128)S(1)}, s32[2048]{0:T(1024)S(1)}, s32[8,2048]{1,0:T(8,128)S(1)}, bf16[8,2048,256]{2,1,0:T(8,128)(2,1)}) %tuple.52), condition=%wide.region_5.6_spmd.clone.clone, body=%wide.region_3.5_spmd.clone.sunk.clone | while | flops 2165311488 | bytes 5309004 | solution.py:26
  306.3 5.1 %fusion.37 = f32[2048,256]{1,0:T(8,128)S(1)} fusion(s32[2048]{0:T(1024)S(1)} %bitcast.64, f32[2048,256]{1,0:T(8,128)S(1)} %get-tuple-element.243, bf16[8,2048,256]{2,1,0:T(8,128)(2,1)} %get-tuple-element.251, s32[]{:T(128)} %get-tuple-element.242, pred[]{:T(512)S(6)} %compare.8), kind=kOutput, calls=%fused_computation.7.clone.1.clone | convolution fusion | flops 2152726528 | bytes 5251585 | tf_op jit(solution)/shard_map/while/body/eval_jaxpr/dot_general | solution.py:19
  311.4 1.7 fusion.38
  313.2 5.0 %fusion.37 = f32[2048,256]{1,0:T(8,128)S(1)} fusion(s32[2048]{0:T(1024)S(1)} %bitcast.64, f32[2048,256]{1,0:T(8,128)S(1)} %get-tuple-element.243, bf16[8,2048,256]{2,1,0:T(8,128)(2,1)} %get-tuple-element.251, s32[]{:T(128)} %get-tuple-element.242, pred[]{:T(512)S(6)} %compare.8), kind=kOutput, calls=%fused_computation.7.clone.1.clone | convolution fusion | flops 2152726528 | bytes 5251585 | tf_op jit(solution)/shard_map/while/body/eval_jaxpr/dot_general | solution.py:19
  318.1 1.7 fusion.38
  319.9 5.0 %fusion.37 = f32[2048,256]{1,0:T(8,128)S(1)} fusion(s32[2048]{0:T(1024)S(1)} %bitcast.64, f32[2048,256]{1,0:T(8,128)S(1)} %get-tuple-element.243, bf16[8,2048,256]{2,1,0:T(8,128)(2,1)} %get-tuple-element.251, s32[]{:T(128)} %get-tuple-element.242, pred[]{:T(512)S(6)} %compare.8), kind=kOutput, calls=%fused_computation.7.clone.1.clone | convolution fusion | flops 2152726528 | bytes 5251585 | tf_op jit(solution)/shard_map/while/body/eval_jaxpr/dot_general | solution.py:19
  324.9 1.7 fusion.38
  326.7 5.0 %fusion.37 = f32[2048,256]{1,0:T(8,128)S(1)} fusion(s32[2048]{0:T(1024)S(1)} %bitcast.64, f32[2048,256]{1,0:T(8,128)S(1)} %get-tuple-element.243, bf16[8,2048,256]{2,1,0:T(8,128)(2,1)} %get-tuple-element.251, s32[]{:T(128)} %get-tuple-element.242, pred[]{:T(512)S(6)} %compare.8), kind=kOutput, calls=%fused_computation.7.clone.1.clone | convolution fusion | flops 2152726528 | bytes 5251585 | tf_op jit(solution)/shard_map/while/body/eval_jaxpr/dot_general | solution.py:19
  331.7 1.7 fusion.38
  333.4 5.0 %fusion.37 = f32[2048,256]{1,0:T(8,128)S(1)} fusion(s32[2048]{0:T(1024)S(1)} %bitcast.64, f32[2048,256]{1,0:T(8,128)S(1)} %get-tuple-element.243, bf16[8,2048,256]{2,1,0:T(8,128)(2,1)} %get-tuple-element.251, s32[]{:T(128)} %get-tuple-element.242, pred[]{:T(512)S(6)} %compare.8), kind=kOutput, calls=%fused_computation.7.clone.1.clone | convolution fusion | flops 2152726528 | bytes 5251585 | tf_op jit(solution)/shard_map/while/body/eval_jaxpr/dot_general | solution.py:19
  338.4 1.7 fusion.38
  340.2 5.0 %fusion.37 = f32[2048,256]{1,0:T(8,128)S(1)} fusion(s32[2048]{0:T(1024)S(1)} %bitcast.64, f32[2048,256]{1,0:T(8,128)S(1)} %get-tuple-element.243, bf16[8,2048,256]{2,1,0:T(8,128)(2,1)} %get-tuple-element.251, s32[]{:T(128)} %get-tuple-element.242, pred[]{:T(512)S(6)} %compare.8), kind=kOutput, calls=%fused_computation.7.clone.1.clone | convolution fusion | flops 2152726528 | bytes 5251585 | tf_op jit(solution)/shard_map/while/body/eval_jaxpr/dot_general | solution.py:19
  345.2 1.7 fusion.38
  347.0 5.0 %fusion.37 = f32[2048,256]{1,0:T(8,128)S(1)} fusion(s32[2048]{0:T(1024)S(1)} %bitcast.64, f32[2048,256]{1,0:T(8,128)S(1)} %get-tuple-element.243, bf16[8,2048,256]{2,1,0:T(8,128)(2,1)} %get-tuple-element.251, s32[]{:T(128)} %get-tuple-element.242, pred[]{:T(512)S(6)} %compare.8), kind=kOutput, calls=%fused_computation.7.clone.1.clone | convolution fusion | flops 2152726528 | bytes 5251585 | tf_op jit(solution)/shard_map/while/body/eval_jaxpr/dot_general | solution.py:19
  352.0 1.7 fusion.38
  353.7 5.0 %fusion.37 = f32[2048,256]{1,0:T(8,128)S(1)} fusion(s32[2048]{0:T(1024)S(1)} %bitcast.64, f32[2048,256]{1,0:T(8,128)S(1)} %get-tuple-element.243, bf16[8,2048,256]{2,1,0:T(8,128)(2,1)} %get-tuple-element.251, s32[]{:T(128)} %get-tuple-element.242, pred[]{:T(512)S(6)} %compare.8), kind=kOutput, calls=%fused_computation.7.clone.1.clone | convolution fusion | flops 2152726528 | bytes 5251585 | tf_op jit(solution)/shard_map/while/body/eval_jaxpr/dot_general | solution.py:19
  358.7 1.7 fusion.38
  361.9 7.4 %fusion.14 = bf16[4096,256]{1,0:T(8,128)(2,1)} fusion(bf16[2048,256]{1,0:T(8,128)(2,1)S(1)} %divide_convert_fusion, s32[2048]{0:T(1024)S(1)} %get-tuple-element.119), kind=kOutput, calls=%fused_computation.19 | convolution fusion | flops 4304404480 | bytes 3153920 | tf_op jit(solution)/shard_map/dot_general | solution.py:80
  369.3 7.3 %all-to-all-start.3 = ((bf16[32,128,256]{2,1,0:T(8,128)(2,1)}), bf16[32,128,256]{2,1,0:T(8,128)(2,1)S(1)}, u32[]{:S(2)}, u32[]{:S(2)}) async-start(bf16[32,128,256]{2,1,0:T(8,128)(2,1)} %bitcast.13), calls=%async_computation.3 | async-start | bytes 4194304 | tf_op jit(solution)/shard_map/all_to_all | solution.py:88
  377.2 28.4 %all-to-all-done.3 = bf16[32,128,256]{2,1,0:T(8,128)(2,1)S(1)} async-done(((bf16[32,128,256]{2,1,0:T(8,128)(2,1)}), bf16[32,128,256]{2,1,0:T(8,128)(2,1)S(1)}, u32[]{:S(2)}, u32[]{:S(2)}) %all-to-all-start.3) | async-done | bytes 2097184 | tf_op jit(solution)/shard_map/all_to_all | solution.py:88
  406.4 20.1 %all_to_all.33 = f32[4,256,256]{2,1,0:T(8,128)S(1)} all-to-all(f32[4,256,256]{2,1,0:T(8,128)S(1)} %stack.2), channel_id=1, replica_groups=mesh['rows'=32,'grp'=4] {'grp'}, dimensions={0} | all-to-all | bytes 2097152 | tf_op jit(solution)/shard_map/all_to_all | solution.py:114
  (173 shorter events, 58.2 us)
Async XLA Ops:
  3.0 151.5 %copy-start.3 = (s32[1,32]{1,0:T(1,128)S(1)}, s32[1,32]{1,0:T(1,128)}, u32[]{:S(2)}) copy-start(s32[1,32]{1,0:T(1,128)} %param.12) | copy-start | bytes 388
  155.3 15.6 %all-to-all-start = ((s32[32,1,512]{2,1,0:T(1,128)}), s32[32,1,512]{2,1,0:T(1,128)S(1)}, u32[]{:S(2)}, u32[]{:S(2)}) async-start(s32[32,1,512]{2,1,0:T(1,128)} %all_to_all.21), calls=%async_computation | async-start | bytes 131072 | tf_op jit(solution)/shard_map/all_to_all | solution.py:63
  170.8 7.7 %copy-start.2 = (s32[2048]{0:T(1024)S(1)}, s32[2048]{0:T(1024)}, u32[]{:S(2)}) copy-start(s32[2048]{0:T(1024)} %param.14) | copy-start | bytes 24580
  170.9 121.2 %all-to-all-start.1 = ((bf16[32,512,256]{2,1,0:T(8,128)(2,1)}), bf16[32,512,256]{2,1,0:T(8,128)(2,1)}, u32[]{:S(2)}, u32[]{:S(2)}) async-start(bf16[32,512,256]{2,1,0:T(8,128)(2,1)} %broadcast_select_fusion), calls=%async_computation.1 | async-start | bytes 16777216 | tf_op jit(solution)/shard_map/all_to_all | solution.py:62
  292.0 77.3 %all-to-all-start.2 = ((s32[32,1,128]{2,1,0:T(1,128)}), s32[32,1,128]{2,1,0:T(1,128)S(1)}, u32[]{:S(2)}, u32[]{:S(2)}) async-start(s32[32,1,128]{2,1,0:T(1,128)} %bitcast.11), calls=%async_computation.2 | async-start | bytes 32768 | tf_op jit(solution)/shard_map/all_to_all | solution.py:95
  306.3 54.2 %copy-start = (bf16[2048,256]{1,0:T(8,128)(2,1)S(1)}, bf16[2048,256]{1,0:T(8,128)(2,1)}, u32[]{:S(2)}) copy-start(bf16[2048,256]{1,0:T(8,128)(2,1)} %param.13) | copy-start | bytes 3145732
  360.9 1.0 copy-start.1
  369.3 36.3 %copy-start.4 = (bf16[256,256]{1,0:T(8,128)(2,1)S(1)}, bf16[256,256]{1,0:T(8,128)(2,1)}, u32[]{:S(2)}) copy-start(bf16[256,256]{1,0:T(8,128)(2,1)} %param.15) | copy-start | bytes 393220
  369.3 36.3 %all-to-all-start.3 = ((bf16[32,128,256]{2,1,0:T(8,128)(2,1)}), bf16[32,128,256]{2,1,0:T(8,128)(2,1)S(1)}, u32[]{:S(2)}, u32[]{:S(2)}) async-start(bf16[32,128,256]{2,1,0:T(8,128)(2,1)} %bitcast.13), calls=%async_computation.3 | async-start | bytes 4194304 | tf_op jit(solution)/shard_map/all_to_all | solution.py:88
